TPU v7x, 128 devices: a whole 4x4x4 slice. The times are simulated.
128 devices in a mesh: grow: 8 (over x_lo, y), gcol: 16 (over z, x_hi, core).
Axes of the slice: x: 4 (x_hi: 2, x_lo: 2; x = x_hi * 2 + x_lo), y: 4, z: 4, core: 2. Of those that a mesh axis runs over, the one named last changes fastest.
Arguments:
- screened: bfloat16 [2, 16384, 16384], P(None, 'grow', 'gcol'), may hold values from -6 to 6
- elements: bfloat16 [2, 1024, 16384], P(None, None, ('grow', 'gcol')), may hold values from -0.046875 to 0.046875
- energy_grid: float32 [256], replicated, may hold values from -3 to 3
- band_index: int32 [256], replicated, may hold values from 0 to 255
- energy_index: int32 [4, 16], replicated, may hold values from 0 to 255
Outputs:
- sigma: float32 [2, 4, 16], replicated
All inputs are finite; a program needn't handle non-finite values.
Results may differ from a plain program's by a relative error of at most 0.0003.
Values may be sent and summed in bfloat16 or wider, within the bound.
No kernel may reach another device: no remote copies, remote signals or barrier semaphores. Data moves between devices by JAX's collectives and lax.ppermute only.
A program may use at most 128 MiB of HBM per device.

v0:
```python
import jax
import jax.numpy as jnp
from jax import lax
from jax.sharding import PartitionSpec as P


def spread(block, axis, source):
    block = jnp.where(lax.axis_index(axis) == source, block, jnp.zeros_like(block))
    return lax.psum(block, axis)


def weights(energy_grid, band_index, energy_index):
    points = lax.broadcasted_iota(jnp.int32, (1, energy_grid.shape[0]), 1)
    band_energy = jnp.sum(
        jnp.where(band_index[:, None] == points, energy_grid[None, :], 0.0), axis=-1
    )
    eval_energy = jnp.sum(
        jnp.where(energy_index[:, :, None] == points[None], energy_grid[None, None, :], 0.0),
        axis=-1,
    )
    offset = eval_energy[:, None, :] - band_energy[None, :, None]
    denom = offset * offset + 0.25
    return (offset / denom, -0.5 / denom)


def weigh(s_re, s_im, wre, wim):
    outer = wre.shape[0]
    summed = wre.shape[1]
    sre = s_re.reshape(outer, summed)[:, :, None]
    sim = s_im.reshape(outer, summed)[:, :, None]
    scale = summed ** (-0.5)
    out_re = scale * jnp.sum(wre * sre - wim * sim, axis=1)
    out_im = scale * jnp.sum(wre * sim + wim * sre, axis=1)
    return (out_re, out_im)


def local(screened, elements, energy_grid, band_index, energy_index):
    row_part = lax.all_gather(elements, "gcol", axis=2, tiled=True)
    ncol = screened.shape[2]
    place = lax.axis_index("gcol")
    half = lax.dynamic_slice_in_dim(row_part, place % 2 * ncol, ncol, 2)
    col_part = spread(half, "grow", place // 2)
    prod = jnp.einsum("mph,wgh->mpwg", col_part, screened, preferred_element_type=jnp.float32)
    yre = prod[0, :, 0] - prod[1, :, 1]
    yim = prod[1, :, 0] + prod[0, :, 1]
    rre = row_part[0].astype(jnp.float32)
    rim = row_part[1].astype(jnp.float32)
    s_re = jnp.sum(rre * yre + rim * yim, axis=-1)
    s_im = jnp.sum(rre * yim - rim * yre, axis=-1)
    wre, wim = weights(energy_grid, band_index, energy_index)
    total_re, total_im = lax.psum((s_re, s_im), ("grow", "gcol"))
    out_re, out_im = weigh(total_re, total_im, wre, wim)
    return jnp.stack([out_re, out_im])


def solution(mesh):
    in_specs = (P(None, "grow", "gcol"), P(None, None, ("grow", "gcol")), P(), P(), P())
    out_specs = P()
    return jax.shard_map(local, mesh=mesh, in_specs=in_specs, out_specs=out_specs, check_vma=False)
```

profile of v0, /device:TPU:1, one launch (start us, length us, event | category | flops | bytes accessed | tf_op | source)
XLA Modules:
  0.0 312.0 jit_solution(5005722360260161644)
XLA Ops:
  6.5 0.0 copy-start
  6.5 0.0 copy-start.1
  6.5 0.0 copy-start.2
  6.5 0.0 all-gather.2.cloned.1.call-start
  6.5 0.7 all-gather.2.cloned.1.call-update
  7.3 0.0 all-reduce.3.cloned.1.call-start
  7.3 83.3 %all-gather.2.cloned.1.call-done = bf16[2,1024,2048]{2,1,0:T(8,128)(2,1)} async-done(((bf16[2,1024,128]{2,1,0:T(8,128)(2,1)}), bf16[2,1024,2048]{2,1,0:T(8,128)(2,1)}) %all-gather.2.cloned.1.call-update) | async-done | bytes 8388624 | tf_op jit(solution)/shard_map/all_gather | solution.py:38
  90.6 5.4 %dynamic-slice_select_fusion = bf16[2,1024,1024]{2,1,0:T(8,128)(2,1)} fusion(bf16[2,1024,2048]{2,1,0:T(8,128)(2,1)} %all-gather.2.cloned.1.call-done, s32[]{:T(128)S(6)} %select_n.35, pred[]{:T(512)S(6)} %eq.37), kind=kLoop, calls=%fused_computation.17 | loop fusion | flops 2097152 | bytes 8388613 | tf_op jit(solution)/shard_map/jit(_where)/select_n | solution.py:8
  96.0 0.0 all-reduce.3.cloned.1.call-update
  96.0 0.0 copy-done
  96.1 0.0 copy-done.1
  96.1 0.2 select_reduce_fusion.1
  96.2 0.0 copy-done.2
  96.2 0.2 select_reduce_fusion
  96.4 102.1 %all-reduce.3.cloned.1.call-done = bf16[2,1024,1024]{2,1,0:T(8,128)(2,1)} async-done(((bf16[2,1024,1024]{2,1,0:T(8,128)(2,1)}), bf16[2,1024,1024]{2,1,0:T(8,128)(2,1)}) %all-reduce.3.cloned.1.call-update) | async-done | bytes 4194320 | tf_op jit(solution)/shard_map/psum | solution.py:9
  198.5 25.1 %fusion.6 = f32[2,1024,2,2048]{3,1,2,0:T(8,128)} fusion(bf16[2,2048,1024]{2,1,0:T(8,128)(2,1)} %param.5, bf16[2,1024,1024]{2,1,0:T(8,128)(2,1)} %all-reduce.3.cloned.1.call-done), kind=kOutput, calls=%fused_computation.12 | convolution fusion | flops 17179869184 | bytes 46137344 | tf_op jit(solution)/shard_map/mph,wgh->mpwg/dot_general | solution.py:43
  223.6 16.1 %fusion.1 = (f32[1024]{0:T(1024)S(1)}, f32[1024]{0:T(1024)S(1)}) fusion(bf16[2,1024,2048]{2,1,0:T(8,128)(2,1)} %all-gather.2.cloned.1.call-done, f32[2,1024,2,2048]{3,1,2,0:T(8,128)} %fusion.6), kind=kLoop, calls=%fused_computation.5 | loop fusion | flops 25163776 | bytes 41951232 | tf_op jit(solution)/shard_map/reduce_sum | solution.py:48
  239.7 64.7 %all-reduce = (f32[4,256]{1,0:T(4,128)S(1)}, f32[4,256]{1,0:T(4,128)S(1)}) all-reduce(f32[4,256]{1,0:T(4,128)S(1)} %mul.85, f32[4,256]{1,0:T(4,128)S(1)} %mul.80), channel_id=1, replica_groups=mesh['grow'=8,'gcol'=16] {'grow','gcol'}, use_global_device_ids=true, to_apply=%region_6.7 | all-reduce | flops 2048 | bytes 16384 | tf_op jit(solution)/shard_map/psum | solution.py:51
  304.4 0.2 subtract_reduce_fusion
  304.6 0.6 pad_maximum_fusion
  (3 shorter events, 0.0 us)
Async XLA Ops:
  6.5 89.5 %copy-start = (f32[256]{0:T(256)S(1)}, f32[256]{0:T(256)}, u32[]{:S(2)}) copy-start(f32[256]{0:T(256)} %param.7) | copy-start | bytes 3076
  6.5 89.5 %copy-start.1 = (s32[4,16]{1,0:T(4,128)S(1)}, s32[4,16]{1,0:T(4,128)}, u32[]{:S(2)}) copy-start(s32[4,16]{1,0:T(4,128)} %param.9) | copy-start | bytes 772
  6.5 89.7 %copy-start.2 = (s32[256]{0:T(256)S(1)}, s32[256]{0:T(256)}, u32[]{:S(2)}) copy-start(s32[256]{0:T(256)} %param.8) | copy-start | bytes 3076
  6.5 84.1 %all-gather.2.cloned.1.call-start = ((), (), s32[]{:S(2)}) async-start(), calls=%async_computation | async-start | bytes 8912896 | tf_op jit(solution)/shard_map/all_gather | solution.py:38
  7.3 191.2 %all-reduce.3.cloned.1.call-start = ((), (), s32[]{:S(2)}) async-start(), calls=%async_computation.1 | async-start | bytes 8388608 | tf_op jit(solution)/shard_map/psum | solution.py:9
Sparse Core Ops, SparseCore 0:
  9.7 80.8 all-gather.1
  96.2 102.2 all-reduce.2
where the time goes:
time: 312 us
  waiting for transfers between devices  186 us (60%)
  blocking collectives  64.7 us (21%)
  matrix products  25.1 us (8%)
  other arithmetic  22.6 us (7%)
  between operations  13.5 us (4%)
    psum x1, waiting for transfers between devices, spread(): return lax.psum(block, axis)  102 us
    all_gather x1, waiting for transfers between devices, local(): row_part = lax.all_gather(elements, 'gcol', axis=2, tiled=True)  83.3 us
    psum x1, blocking collectives, local(): total_re, total_im = lax.psum((s_re, s_im), ('grow', 'gcol'))  64.7 us
    dot_general x1, matrix products, local(): jnp.einsum('mph,wgh->mpwg', col_part, screened, preferred_element_type=jn...  25.1 us
    reduce_sum x1, other arithmetic, local(): s_re = jnp.sum(rre * yre + rim * yim, axis=-1)  16.1 us
  transfers between devices with their start and end apart: 2, of which 2 were waited for; matrix products, arithmetic and copies ran while one was open for 0% of the time, Pallas kernels for 0%

commit v1 on v0

--- a/solution.py
+++ b/solution.py
@@ -48,7 +48,7 @@
     s_re = jnp.sum(rre * yre + rim * yim, axis=-1)
     s_im = jnp.sum(rre * yim - rim * yre, axis=-1)
     wre, wim = weights(energy_grid, band_index, energy_index)
-    total_re, total_im = lax.psum((s_re, s_im), ("grow", "gcol"))
+    total_re, total_im = lax.psum(lax.psum((s_re, s_im), "gcol"), "grow")
     out_re, out_im = weigh(total_re, total_im, wre, wim)
     return jnp.stack([out_re, out_im])
 

time: 312 us -> 302 us (0.968)
  the two profiles are of different devices: /device:TPU:1 before, /device:TPU:8 now
where the time goes in v1:
time: 302 us; the launch traced here: 301 us
  waiting for transfers between devices  183 us (61%)
  blocking collectives  57.1 us (19%)
  matrix products  25.1 us (8%)
  other arithmetic  22.6 us (7%)
  between operations  13.5 us (4%)
    psum x1, waiting for transfers between devices, spread(): return lax.psum(block, axis)  100 us
    all_gather x1, waiting for transfers between devices, local(): row_part = lax.all_gather(elements, 'gcol', axis=2, tiled=True)  81.9 us
    psum x2, blocking collectives, local(): total_re, total_im = lax.psum(lax.psum((s_re, s_im), 'gcol'), 'grow')  57.1 us
    dot_general x1, matrix products, local(): jnp.einsum('mph,wgh->mpwg', col_part, screened, preferred_element_type=jn...  25.1 us
    reduce_sum x1, other arithmetic, local(): s_re = jnp.sum(rre * yre + rim * yim, axis=-1)  16.1 us
  transfers between devices with their start and end apart: 2, of which 2 were waited for; matrix products, arithmetic and copies ran while one was open for 0% of the time, Pallas kernels for 0%

profile of v1, /device:TPU:8, one launch (start us, length us, event | category | flops | bytes accessed | tf_op | source)
XLA Modules:
  0.0 301.4 jit_solution(10370458647661979691)
XLA Ops:
  6.5 0.0 copy-start
  6.5 0.0 copy-start.1
  6.5 0.0 copy-start.2
  6.5 0.0 all-gather.2.cloned.1.call-start
  6.5 0.7 all-gather.2.cloned.1.call-update
  7.3 0.0 all-reduce.4.cloned.1.call-start
  7.3 81.9 %all-gather.2.cloned.1.call-done = bf16[2,1024,2048]{2,1,0:T(8,128)(2,1)} async-done(((bf16[2,1024,128]{2,1,0:T(8,128)(2,1)}), bf16[2,1024,2048]{2,1,0:T(8,128)(2,1)}) %all-gather.2.cloned.1.call-update) | async-done | bytes 8388624 | tf_op jit(solution)/shard_map/all_gather | solution.py:38
  89.3 5.4 %dynamic-slice_select_fusion = bf16[2,1024,1024]{2,1,0:T(8,128)(2,1)} fusion(bf16[2,1024,2048]{2,1,0:T(8,128)(2,1)} %all-gather.2.cloned.1.call-done, s32[]{:T(128)S(6)} %select_n.35, pred[]{:T(512)S(6)} %eq.37), kind=kLoop, calls=%fused_computation.17 | loop fusion | flops 2097152 | bytes 8388613 | tf_op jit(solution)/shard_map/jit(_where)/select_n | solution.py:8
  94.7 0.0 all-reduce.4.cloned.1.call-update
  94.7 0.0 copy-done
  94.7 0.0 copy-done.1
  94.7 0.2 select_reduce_fusion.1
  94.9 0.0 copy-done.2
  94.9 0.2 select_reduce_fusion
  95.1 100.4 %all-reduce.4.cloned.1.call-done = bf16[2,1024,1024]{2,1,0:T(8,128)(2,1)} async-done(((bf16[2,1024,1024]{2,1,0:T(8,128)(2,1)}), bf16[2,1024,1024]{2,1,0:T(8,128)(2,1)}) %all-reduce.4.cloned.1.call-update) | async-done | bytes 4194320 | tf_op jit(solution)/shard_map/psum | solution.py:9
  195.5 25.1 %fusion.6 = f32[2,1024,2,2048]{3,1,2,0:T(8,128)} fusion(bf16[2,2048,1024]{2,1,0:T(8,128)(2,1)} %param.5, bf16[2,1024,1024]{2,1,0:T(8,128)(2,1)} %all-reduce.4.cloned.1.call-done), kind=kOutput, calls=%fused_computation.12 | convolution fusion | flops 17179869184 | bytes 46137344 | tf_op jit(solution)/shard_map/mph,wgh->mpwg/dot_general | solution.py:43
  220.6 16.1 %fusion.1 = (f32[1024]{0:T(1024)S(1)}, f32[1024]{0:T(1024)S(1)}) fusion(bf16[2,1024,2048]{2,1,0:T(8,128)(2,1)} %all-gather.2.cloned.1.call-done, f32[2,1024,2,2048]{3,1,2,0:T(8,128)} %fusion.6), kind=kLoop, calls=%fused_computation.5 | loop fusion | flops 25163776 | bytes 41951232 | tf_op jit(solution)/shard_map/reduce_sum | solution.py:48
  236.7 38.5 %all-reduce = (f32[1024]{0:T(1024)S(1)}, f32[1024]{0:T(1024)S(1)}) all-reduce(f32[1024]{0:T(1024)S(1)} %get-tuple-element.6, f32[1024]{0:T(1024)S(1)} %get-tuple-element.5), channel_id=1, replica_groups=mesh['grow'=8,'gcol'=16] {'gcol'}, use_global_device_ids=true, to_apply=%region_7.8 | all-reduce | flops 2048 | bytes 16384 | tf_op jit(solution)/shard_map/psum | solution.py:51
  275.2 18.6 %all-reduce.1 = (f32[4,256]{1,0:T(4,128)S(1)}, f32[4,256]{1,0:T(4,128)S(1)}) all-reduce(f32[4,256]{1,0:T(4,128)S(1)} %mul.85, f32[4,256]{1,0:T(4,128)S(1)} %mul.80), channel_id=1, replica_groups=mesh['grow'=8,'gcol'=16] {'grow'}, use_global_device_ids=true, to_apply=%region_8.9 | all-reduce | flops 2048 | bytes 16384 | tf_op jit(solution)/shard_map/psum | solution.py:51
  293.8 0.2 subtract_reduce_fusion
  294.0 0.6 pad_maximum_fusion
  (3 shorter events, 0.0 us)
Async XLA Ops:
  6.5 88.2 %copy-start = (f32[256]{0:T(256)S(1)}, f32[256]{0:T(256)}, u32[]{:S(2)}) copy-start(f32[256]{0:T(256)} %param.7) | copy-start | bytes 3076
  6.5 88.2 %copy-start.1 = (s32[4,16]{1,0:T(4,128)S(1)}, s32[4,16]{1,0:T(4,128)}, u32[]{:S(2)}) copy-start(s32[4,16]{1,0:T(4,128)} %param.9) | copy-start | bytes 772
  6.5 88.3 %copy-start.2 = (s32[256]{0:T(256)S(1)}, s32[256]{0:T(256)}, u32[]{:S(2)}) copy-start(s32[256]{0:T(256)} %param.8) | copy-start | bytes 3076
  6.5 82.7 %all-gather.2.cloned.1.call-start = ((), (), s32[]{:S(2)}) async-start(), calls=%async_computation | async-start | bytes 8912896 | tf_op jit(solution)/shard_map/all_gather | solution.py:38
  7.3 188.2 %all-reduce.4.cloned.1.call-start = ((), (), s32[]{:S(2)}) async-start(), calls=%async_computation.1 | async-start | bytes 8388608 | tf_op jit(solution)/shard_map/psum | solution.py:9
Sparse Core Ops, SparseCore 0:
  9.7 79.5 all-gather.1
  94.8 100.6 all-reduce.3

commit v2 on v0

--- a/solution.py
+++ b/solution.py
@@ -35,7 +35,9 @@
 
 
 def local(screened, elements, energy_grid, band_index, energy_index):
-    row_part = lax.all_gather(elements, "gcol", axis=2, tiled=True)
+    row_part = jnp.concatenate(
+        lax.all_to_all(jnp.stack([elements] * lax.axis_size("gcol")), "gcol", 0, 0), axis=2
+    )
     ncol = screened.shape[2]
     place = lax.axis_index("gcol")
     half = lax.dynamic_slice_in_dim(row_part, place % 2 * ncol, ncol, 2)

time: 312 us -> 374 us (1.20)
  local copies, waits for them, and re-layouts: 0.03 us -> 24.8 us
  other arithmetic: 22.6 us -> 36.8 us
  waiting for transfers between devices: 186 us -> 199 us
  starting transfers between devices: 0.04 us -> 9.33 us
    all_to_all x0 -> x1, waiting for transfers between devices: none -> 96 us  [local(): lax.all_to_all(jnp.stack([elements] * lax.axis_size('gcol')), 'gcol', 0, 0)]
    all_gather x1 -> x0, waiting for transfers between devices: 83.3 us -> none  [local(): row_part = lax.all_gather(elements, 'gcol', axis=2, tiled=True)]
    unnamed x0 -> x1, other arithmetic: none -> 19.1 us
    unnamed x6 -> x8, local copies, waits for them, and re-layouts: 0.01 us -> 10.8 us
    all_to_all x0 -> x1, starting transfers between devices: none -> 9.29 us  [local(): lax.all_to_all(jnp.stack([elements] * lax.axis_size('gcol')), 'gcol', 0, 0)]
    reshape x0 -> x1, local copies, waits for them, and re-layouts: none -> 7.85 us  [local(): jnp.concatenate(lax.all_to_all(jnp.stack([elements] * lax.axis_size('gcol...]
    another operation x0 -> x1, local copies, waits for them, and re-layouts: none -> 6.2 us  [local(): jnp.stack([elements] * lax.axis_size('gcol'))]
    reduce_sum x1, other arithmetic: 16.1 us -> 11.1 us  [local(): s_re = jnp.sum(rre * yre + rim * yim, axis=-1)]
where the time goes in v2:
time: 374 us; the launch traced here: 373 us
  waiting for transfers between devices  199 us (53%)
  blocking collectives  64.7 us (17%)
  other arithmetic  36.8 us (10%)
  matrix products  25.1 us (7%)
  local copies, waits for them, and re-layouts  24.8 us (7%)
  between operations  13.5 us (4%)
  starting transfers between devices  9.33 us (2%)
    psum x1, waiting for transfers between devices, spread(): return lax.psum(block, axis)  103 us
    all_to_all x1, waiting for transfers between devices, local(): lax.all_to_all(jnp.stack([elements] * lax.axis_size('gcol')), 'gcol', 0, 0)  96 us
    psum x1, blocking collectives, local(): total_re, total_im = lax.psum((s_re, s_im), ('grow', 'gcol'))  64.7 us
    dot_general x1, matrix products, local(): jnp.einsum('mph,wgh->mpwg', col_part, screened, preferred_element_type=jn...  25.1 us
    unnamed x1, other arithmetic  19.1 us
    reduce_sum x1, other arithmetic, local(): s_re = jnp.sum(rre * yre + rim * yim, axis=-1)  11.1 us
    unnamed x8, local copies, waits for them, and re-layouts  10.8 us
    all_to_all x1, starting transfers between devices, local(): lax.all_to_all(jnp.stack([elements] * lax.axis_size('gcol')), 'gcol', 0, 0)  9.29 us
  transfers between devices with their start and end apart: 2, of which 2 were waited for; matrix products, arithmetic and copies ran while one was open for 0% of the time, Pallas kernels for 0%

profile of v2, /device:TPU:1, one launch (start us, length us, event | category | flops | bytes accessed | tf_op | source)
XLA Modules:
  0.0 373.2 jit_solution(4543142150673921016)
XLA Ops:
  6.5 6.2 %stack.4 = bf16[16,2,1024,128]{3,2,1,0:T(8,128)(2,1)} broadcast(bf16[2,1024,128]{2,1,0:T(8,128)(2,1)} %param.6), dimensions={1,2,3} | broadcast | bytes 8912896 | tf_op jit(solution)/shard_map/stack | solution.py:39
  12.7 9.3 %all-to-all-start = ((bf16[16,2,1024,128]{3,2,1,0:T(8,128)(2,1)}), bf16[16,2,1024,128]{3,2,1,0:T(8,128)(2,1)}, u32[]{:S(2)}, u32[]{:S(2)}) async-start(bf16[16,2,1024,128]{3,2,1,0:T(8,128)(2,1)} %stack.4), calls=%async_computation | async-start | bytes 16777216 | tf_op jit(solution)/shard_map/all_to_all | solution.py:39
  22.0 0.0 all-reduce.3.cloned.1.call-start
  22.1 96.0 %all-to-all-done = bf16[16,2,1024,128]{3,2,1,0:T(8,128)(2,1)} async-done(((bf16[16,2,1024,128]{3,2,1,0:T(8,128)(2,1)}), bf16[16,2,1024,128]{3,2,1,0:T(8,128)(2,1)}, u32[]{:S(2)}, u32[]{:S(2)}) %all-to-all-start) | async-done | bytes 8388640 | tf_op jit(solution)/shard_map/all_to_all | solution.py:39
  118.1 7.8 %copy_bitcast_fusion = bf16[2,1024,2048]{2,1,0:T(8,128)(2,1)} fusion(bf16[16,2,1024,128]{3,2,1,0:T(8,128)(2,1)} %all-to-all-done), kind=kLoop, calls=%fused_computation.8 | loop fusion | bytes 16777216 | tf_op jit(solution)/shard_map/reshape | solution.py:38
  125.9 0.0 copy-start
  125.9 0.0 copy-start.1
  125.9 0.0 copy-start.2
  125.9 5.5 %dynamic-slice_select_fusion = bf16[2,1024,1024]{2,1,0:T(8,128)(2,1)} fusion(bf16[2,1024,2048]{2,1,0:T(8,128)(2,1)} %copy_bitcast_fusion, s32[]{:T(128)S(6)} %select_n.35, pred[]{:T(512)S(6)} %eq.37), kind=kLoop, calls=%fused_computation.16 | loop fusion | flops 2097152 | bytes 8388613 | tf_op jit(solution)/shard_map/jit(_where)/select_n | solution.py:8
  131.4 0.0 all-reduce.3.cloned.1.call-update
  131.4 0.0 copy-done
  131.4 0.0 copy-done.1
  131.4 0.2 select_reduce_fusion.1
  131.6 0.0 copy-done.2
  131.6 0.2 select_reduce_fusion
  131.8 103.0 %all-reduce.3.cloned.1.call-done = bf16[2,1024,1024]{2,1,0:T(8,128)(2,1)} async-done(((bf16[2,1024,1024]{2,1,0:T(8,128)(2,1)}), bf16[2,1024,1024]{2,1,0:T(8,128)(2,1)}) %all-reduce.3.cloned.1.call-update) | async-done | bytes 4194320 | tf_op jit(solution)/shard_map/psum | solution.py:9
  234.8 25.1 %fusion.6 = f32[2,1024,2,2048]{3,1,2,0:T(8,128)} fusion(bf16[2,2048,1024]{2,1,0:T(8,128)(2,1)} %param.5, bf16[2,1024,1024]{2,1,0:T(8,128)(2,1)} %all-reduce.3.cloned.1.call-done), kind=kOutput, calls=%fused_computation.13 | convolution fusion | flops 17179869184 | bytes 46137344 | tf_op jit(solution)/shard_map/mph,wgh->mpwg/dot_general | solution.py:45
  259.9 19.1 %fusion.5 = (f32[128,8,16,128]{3,1,2,0:T(8,128)}, f32[128,8,16,128]{3,1,2,0:T(8,128)}) fusion(f32[2,1024,2,2048]{3,1,2,0:T(8,128)} %fusion.6), kind=kLoop, calls=%fused_computation.12 | loop fusion | flops 4194304 | bytes 50331648
  279.0 5.4 %copy.18 = f32[128,8,16,128]{3,2,1,0:T(8,128)S(1)} copy(f32[128,8,16,128]{3,1,2,0:T(8,128)} %get-tuple-element.11) | data formatting | bytes 16777216
  284.4 5.4 %copy.19 = f32[128,8,16,128]{3,2,1,0:T(8,128)S(1)} copy(f32[128,8,16,128]{3,1,2,0:T(8,128)} %get-tuple-element.12) | data formatting | bytes 16777216
  289.7 11.1 %fusion.1 = (f32[1024]{0:T(1024)S(1)}, f32[1024]{0:T(1024)S(1)}) fusion(f32[1,1024,16,128]{3,2,1,0:T(8,128)S(1)} %bitcast.33, f32[1,1024,16,128]{3,2,1,0:T(8,128)S(1)} %bitcast.32, bf16[2,1024,16,128]{3,1,0,2:T(8,128)(2,1)} %bitcast), kind=kLoop, calls=%fused_computation.5 | loop fusion | flops 20969472 | bytes 25174016 | tf_op jit(solution)/shard_map/reduce_sum | solution.py:50
  300.9 64.7 %all-reduce = (f32[4,256]{1,0:T(4,128)S(1)}, f32[4,256]{1,0:T(4,128)S(1)}) all-reduce(f32[4,256]{1,0:T(4,128)S(1)} %mul.89, f32[4,256]{1,0:T(4,128)S(1)} %mul.84), channel_id=1, replica_groups=mesh['grow'=8,'gcol'=16] {'grow','gcol'}, use_global_device_ids=true, to_apply=%region_6.7 | all-reduce | flops 2048 | bytes 16384 | tf_op jit(solution)/shard_map/psum | solution.py:53
  365.6 0.2 subtract_reduce_fusion
  365.8 0.6 pad_maximum_fusion
  (3 shorter events, 0.0 us)
Async XLA Ops:
  12.7 105.3 %all-to-all-start = ((bf16[16,2,1024,128]{3,2,1,0:T(8,128)(2,1)}), bf16[16,2,1024,128]{3,2,1,0:T(8,128)(2,1)}, u32[]{:S(2)}, u32[]{:S(2)}) async-start(bf16[16,2,1024,128]{3,2,1,0:T(8,128)(2,1)} %stack.4), calls=%async_computation | async-start | bytes 16777216 | tf_op jit(solution)/shard_map/all_to_all | solution.py:39
  22.0 212.7 %all-reduce.3.cloned.1.call-start = ((), (), s32[]{:S(2)}) async-start(), calls=%async_computation.1 | async-start | bytes 8388608 | tf_op jit(solution)/shard_map/psum | solution.py:9
  125.9 5.5 %copy-start = (f32[256]{0:T(256)S(1)}, f32[256]{0:T(256)}, u32[]{:S(2)}) copy-start(f32[256]{0:T(256)} %param.7) | copy-start | bytes 3076
  125.9 5.5 %copy-start.1 = (s32[4,16]{1,0:T(4,128)S(1)}, s32[4,16]{1,0:T(4,128)}, u32[]{:S(2)}) copy-start(s32[4,16]{1,0:T(4,128)} %param.9) | copy-start | bytes 772
  125.9 5.7 %copy-start.2 = (s32[256]{0:T(256)S(1)}, s32[256]{0:T(256)}, u32[]{:S(2)}) copy-start(s32[256]{0:T(256)} %param.8) | copy-start | bytes 3076
Sparse Core Ops, SparseCore 0:
  131.5 103.1 all-reduce.2
